TPU v7x, 32 devices: a whole 2x2x4 slice. The times are simulated.
32 devices in a mesh: seq: 4 (over x, core), dp: 8 (over z, y).
Axes of the slice: x: 2, y: 2, z: 4, core: 2. Of those that a mesh axis runs over, the one named last changes fastest.
Arguments:
- tokens: bfloat16 [8, 1280, 960], P('dp', 'seq'), may hold values from -6 to 6
- seg_ids: int32 [8, 1280], P('dp', 'seq'), may hold values from 0 to 4, as said below
- positions: int32 [8, 1280], P('dp', 'seq'), may hold values from 0 to 1279, as said below
- attn_gain: float32 [960], replicated, may hold values from 0.25 to 1.75
- w_query: bfloat16 [960, 960], replicated, may hold values from -0.1875 to 0.1875
- w_key: bfloat16 [960, 320], replicated, may hold values from -0.1875 to 0.1875
- w_value: bfloat16 [960, 320], replicated, may hold values from -0.1875 to 0.1875
- w_out: bfloat16 [960, 960], replicated, may hold values from -0.5 to 0.5
- ffn_gain: float32 [960], replicated, may hold values from 0.25 to 1.75
- w_gate: bfloat16 [960, 2560], P(None, 'seq'), may hold values from -0.1875 to 0.1875
- w_up: bfloat16 [960, 2560], P(None, 'seq'), may hold values from -0.1875 to 0.1875
- w_down: bfloat16 [2560, 960], P('seq'), may hold values from -0.125 to 0.125
- cotangent: bfloat16 [8, 1280, 960], P('dp', 'seq'), may hold values from -6 to 6
Outputs:
- output: bfloat16 [8, 1280, 960], P('dp', 'seq')
- input_grad: float32 [8, 1280, 960], P('dp', 'seq')
- attn_gain_grad: float32 [960], P('dp')
- w_query_grad: float32 [960, 960], P('dp')
- w_key_grad: float32 [960, 320], P('dp')
- w_value_grad: float32 [960, 320], P('dp')
- w_out_grad: float32 [960, 960], P('dp')
- ffn_gain_grad: float32 [960], P('dp')
- w_gate_grad: float32 [960, 2560], P('dp', 'seq')
- w_up_grad: float32 [960, 2560], P('dp', 'seq')
- w_down_grad: float32 [2560, 960], P('seq', 'dp')
Inputs may be any that keep to these rules, and one draw needn't show every extreme that they name: `seg_ids`: within a row the ids start at 0 and never fall. `positions`: A token's position counts the tokens before it in its document (0 at a document's first token).
All inputs are finite; a program needn't handle non-finite values.
Results may differ from a plain program's by a relative error of at most 0.025.
Values may be sent and summed in bfloat16 or wider, within the bound.
A program may use at most 256 MiB of HBM per device.

v0:
```python
import jax
import jax.numpy as jnp
from jax import lax
from jax.sharding import PartitionSpec as P

HEADS = 15
KV_HEADS = 5
HEAD_DIM = 64
EPSILON = 1e-05
THETA = 10000.0
MASKED = -1e30


def rope_tables(positions):
    half_dim = HEAD_DIM // 2
    frequency = THETA ** (-(jnp.arange(half_dim, dtype=jnp.float32) * 2.0 / HEAD_DIM))
    angles = positions.astype(jnp.float32)[..., None] * frequency
    return (jnp.cos(angles), jnp.sin(angles))


def rotate(values, cos_table, sin_table):
    half_dim = values.shape[-1] // 2
    first_half = values[..., :half_dim]
    second_half = values[..., half_dim:]
    cos_head = cos_table[..., None, :]
    sin_head = sin_table[..., None, :]
    return jnp.concatenate(
        [
            first_half * cos_head - second_half * sin_head,
            second_half * cos_head + first_half * sin_head,
        ],
        axis=-1,
    )


def norm_forward(residual, gain_vec):
    inverse = lax.rsqrt(jnp.mean(residual * residual, axis=-1, keepdims=True) + EPSILON)
    return ((residual * inverse * gain_vec).astype(jnp.bfloat16), inverse)


def norm_backward(residual, inverse, gain_vec, upstream):
    weighted = upstream * gain_vec
    inner_mean = jnp.mean(weighted * residual, axis=-1, keepdims=True)
    residual_grad = inverse * weighted - residual * (inverse * inverse * inverse) * inner_mean
    gain_grad = jnp.sum(upstream * residual * inverse, axis=(0, 1))
    return (residual_grad, gain_grad)


def masked_scores(queries, keys_all, allowed):
    raw_scores = jnp.einsum("qkgd,tkd->kgqt", queries, keys_all, preferred_element_type=jnp.float32)
    return jnp.where(allowed[None, None], raw_scores * HEAD_DIM ** (-0.5), MASKED)


def row_attend(operands):
    queries, keys_all, values_all, allowed = operands
    scores = masked_scores(queries, keys_all, allowed)
    row_max = jnp.max(scores, axis=-1, keepdims=True)
    shifted = jnp.exp(scores - row_max)
    row_total = jnp.sum(shifted, axis=-1, keepdims=True)
    probs_low = (shifted / row_total).astype(jnp.bfloat16)
    mixed_heads = jnp.einsum(
        "kgqt,tkd->qkgd", probs_low, values_all, preferred_element_type=jnp.float32
    )
    return (mixed_heads, row_max + jnp.log(row_total))


def row_backward(operands):
    queries, keys_all, values_all, allowed, log_total, mixed_grad = operands
    scores = masked_scores(queries, keys_all, allowed)
    weights_soft = jnp.exp(scores - log_total)
    probs_grad = jnp.einsum(
        "qkgd,tkd->kgqt", mixed_grad, values_all, preferred_element_type=jnp.float32
    )
    row_delta = jnp.sum(probs_grad * weights_soft, axis=-1, keepdims=True)
    score_grad = (weights_soft * (probs_grad - row_delta)).astype(jnp.bfloat16)
    score_scale = HEAD_DIM ** (-0.5)
    query_grad = (
        jnp.einsum("kgqt,tkd->qkgd", score_grad, keys_all, preferred_element_type=jnp.float32)
        * score_scale
    )
    key_grad = (
        jnp.einsum("kgqt,qkgd->tkd", score_grad, queries, preferred_element_type=jnp.float32)
        * score_scale
    )
    value_grad = jnp.einsum(
        "kgqt,qkgd->tkd",
        weights_soft.astype(jnp.bfloat16),
        mixed_grad,
        preferred_element_type=jnp.float32,
    )
    return (query_grad, key_grad, value_grad)


def on_device(
    tokens,
    seg_ids,
    positions,
    attn_gain,
    w_query,
    w_key,
    w_value,
    w_out,
    ffn_gain,
    w_gate,
    w_up,
    w_down,
    cotangent,
):
    row_count, shard_len, model_width = tokens.shape
    row_len = shard_len * lax.axis_size("seq")
    groups = HEADS // KV_HEADS
    kv_width = KV_HEADS * HEAD_DIM
    doc_all = lax.all_gather(seg_ids, "seq", axis=1, tiled=True)
    query_place = lax.axis_index("seq") * shard_len + jnp.arange(shard_len, dtype=jnp.int32)
    key_place = jnp.arange(row_len, dtype=jnp.int32)
    allowed = (seg_ids[:, :, None] == doc_all[:, None, :]) & (
        key_place[None, None, :] <= query_place[None, :, None]
    )
    cos_table, sin_table = rope_tables(positions)
    gate_mat, up_mat, down_mat = (
        lax.all_gather(w_gate, "seq", axis=1, tiled=True),
        lax.all_gather(w_up, "seq", axis=1, tiled=True),
        lax.all_gather(w_down, "seq", axis=0, tiled=True),
    )
    residual = tokens.astype(jnp.float32)
    kept_runs = []
    for repeat in range(2):
        normed, attn_inverse = norm_forward(residual, attn_gain)
        query_pre = jnp.einsum("rcd,de->rce", normed, w_query, preferred_element_type=jnp.float32)
        key_pre = jnp.einsum("rcd,de->rce", normed, w_key, preferred_element_type=jnp.float32)
        value_pre = jnp.einsum("rcd,de->rce", normed, w_value, preferred_element_type=jnp.float32)
        queries = rotate(
            query_pre.reshape(row_count, shard_len, HEADS, HEAD_DIM), cos_table, sin_table
        ).astype(jnp.bfloat16)
        keys_local = rotate(
            key_pre.reshape(row_count, shard_len, KV_HEADS, HEAD_DIM), cos_table, sin_table
        ).astype(jnp.bfloat16)
        joined = jnp.concatenate(
            [keys_local.reshape(row_count, shard_len, kv_width), value_pre.astype(jnp.bfloat16)],
            axis=-1,
        )
        joined_all = lax.all_gather(joined, "seq", axis=1, tiled=True)
        keys_all = joined_all[..., :kv_width].reshape(row_count, row_len, KV_HEADS, HEAD_DIM)
        values_all = joined_all[..., kv_width:].reshape(row_count, row_len, KV_HEADS, HEAD_DIM)
        grouped = queries.reshape(row_count, shard_len, KV_HEADS, groups, HEAD_DIM)
        mixed_heads, log_total = lax.map(row_attend, (grouped, keys_all, values_all, allowed))
        mixed_low = mixed_heads.reshape(row_count, shard_len, HEADS * HEAD_DIM).astype(jnp.bfloat16)
        after_attn = residual + jnp.einsum(
            "rce,ed->rcd", mixed_low, w_out, preferred_element_type=jnp.float32
        )
        normed_two, ffn_inverse = norm_forward(after_attn, ffn_gain)
        gate_pre = jnp.einsum(
            "rtd,df->rtf", normed_two, gate_mat, preferred_element_type=jnp.float32
        )
        up_pre = jnp.einsum("rtd,df->rtf", normed_two, up_mat, preferred_element_type=jnp.float32)
        ffn_hidden = (jax.nn.silu(gate_pre) * up_pre).astype(jnp.bfloat16)
        partial_sum = jnp.einsum(
            "rtf,fd->rtd", ffn_hidden, down_mat, preferred_element_type=jnp.float32
        )
        normed_rows, gate_pre, up_pre, ffn_out = (normed_two, gate_pre, up_pre, partial_sum)
        kept_runs.append(
            (
                residual,
                normed,
                attn_inverse,
                grouped,
                keys_all,
                values_all,
                log_total,
                mixed_low,
                after_attn,
                ffn_inverse,
                normed_rows,
                gate_pre,
                up_pre,
            )
        )
        residual = after_attn + ffn_out
    output = residual.astype(jnp.bfloat16)
    attn_gain_grad = jnp.zeros(attn_gain.shape, jnp.float32)
    ffn_gain_grad = jnp.zeros(ffn_gain.shape, jnp.float32)
    w_query_grad = jnp.zeros(w_query.shape, jnp.float32)
    w_key_grad = jnp.zeros(w_key.shape, jnp.float32)
    w_value_grad = jnp.zeros(w_value.shape, jnp.float32)
    w_out_grad = jnp.zeros(w_out.shape, jnp.float32)
    w_gate_grad = jnp.zeros(gate_mat.shape, jnp.float32)
    w_up_grad = jnp.zeros(up_mat.shape, jnp.float32)
    w_down_grad = jnp.zeros(down_mat.shape, jnp.float32)
    upstream = cotangent.astype(jnp.float32)
    for repeat in (1, 0):
        (
            residual,
            normed,
            attn_inverse,
            grouped,
            keys_all,
            values_all,
            log_total,
            mixed_low,
            after_attn,
            ffn_inverse,
            normed_rows,
            gate_pre,
            up_pre,
        ) = kept_runs[repeat]
        ffn_grad = upstream.astype(jnp.bfloat16)
        sigmoid_gate = jax.nn.sigmoid(gate_pre)
        silu_gate = jax.nn.silu(gate_pre)
        hidden = (silu_gate * up_pre).astype(jnp.bfloat16)
        w_down_grad = w_down_grad + jnp.einsum(
            "rtf,rtd->fd", hidden, ffn_grad, preferred_element_type=jnp.float32
        )
        hidden_grad = jnp.einsum(
            "rtd,fd->rtf", ffn_grad, down_mat, preferred_element_type=jnp.float32
        )
        gate_grad = (
            hidden_grad * up_pre * sigmoid_gate * (1.0 + gate_pre * (1.0 - sigmoid_gate))
        ).astype(jnp.bfloat16)
        up_grad = (hidden_grad * silu_gate).astype(jnp.bfloat16)
        w_gate_grad = w_gate_grad + jnp.einsum(
            "rtd,rtf->df", normed_rows, gate_grad, preferred_element_type=jnp.float32
        )
        w_up_grad = w_up_grad + jnp.einsum(
            "rtd,rtf->df", normed_rows, up_grad, preferred_element_type=jnp.float32
        )
        normed_two_grad = jnp.einsum(
            "rtf,df->rtd", gate_grad, gate_mat, preferred_element_type=jnp.float32
        ) + jnp.einsum("rtf,df->rtd", up_grad, up_mat, preferred_element_type=jnp.float32)
        after_grad, gain_two = norm_backward(after_attn, ffn_inverse, ffn_gain, normed_two_grad)
        after_grad = after_grad + upstream
        ffn_gain_grad = ffn_gain_grad + gain_two
        attn_grad = after_grad.astype(jnp.bfloat16)
        w_out_grad = w_out_grad + jnp.einsum(
            "rce,rcd->ed", mixed_low, attn_grad, preferred_element_type=jnp.float32
        )
        mixed_grad = jnp.einsum(
            "rcd,ed->rce", attn_grad, w_out, preferred_element_type=jnp.float32
        ).astype(jnp.bfloat16)
        mixed_grad = mixed_grad.reshape(row_count, shard_len, KV_HEADS, groups, HEAD_DIM)
        query_grad, key_grad, value_grad = lax.map(
            row_backward, (grouped, keys_all, values_all, allowed, log_total, mixed_grad)
        )
        joined_grad = jnp.concatenate(
            [
                key_grad.reshape(row_count, row_len, kv_width),
                value_grad.reshape(row_count, row_len, kv_width),
            ],
            axis=-1,
        )
        local_grad = lax.psum_scatter(
            joined_grad.astype(jnp.bfloat16), "seq", scatter_dimension=1, tiled=True
        ).astype(jnp.float32)
        key_back = rotate(
            local_grad[..., :kv_width].reshape(row_count, shard_len, KV_HEADS, HEAD_DIM),
            cos_table,
            -sin_table,
        )
        key_back = key_back.reshape(row_count, shard_len, kv_width).astype(jnp.bfloat16)
        value_back = local_grad[..., kv_width:].astype(jnp.bfloat16)
        query_back = rotate(
            query_grad.reshape(row_count, shard_len, HEADS, HEAD_DIM), cos_table, -sin_table
        )
        query_back = query_back.reshape(row_count, shard_len, HEADS * HEAD_DIM).astype(jnp.bfloat16)
        w_query_grad = w_query_grad + jnp.einsum(
            "rcd,rce->de", normed, query_back, preferred_element_type=jnp.float32
        )
        w_key_grad = w_key_grad + jnp.einsum(
            "rcd,rce->de", normed, key_back, preferred_element_type=jnp.float32
        )
        w_value_grad = w_value_grad + jnp.einsum(
            "rcd,rce->de", normed, value_back, preferred_element_type=jnp.float32
        )
        normed_grad = jnp.einsum(
            "rce,de->rcd", query_back, w_query, preferred_element_type=jnp.float32
        )
        normed_grad = normed_grad + jnp.einsum(
            "rce,de->rcd", key_back, w_key, preferred_element_type=jnp.float32
        )
        normed_grad = normed_grad + jnp.einsum(
            "rce,de->rcd", value_back, w_value, preferred_element_type=jnp.float32
        )
        residual_grad, gain_one = norm_backward(residual, attn_inverse, attn_gain, normed_grad)
        attn_gain_grad = attn_gain_grad + gain_one
        upstream = residual_grad + after_grad
    w_gate_grad, w_up_grad, w_down_grad = (
        lax.psum_scatter(
            w_gate_grad.astype(jnp.bfloat16), "seq", scatter_dimension=1, tiled=True
        ).astype(jnp.float32),
        lax.psum_scatter(
            w_up_grad.astype(jnp.bfloat16), "seq", scatter_dimension=1, tiled=True
        ).astype(jnp.float32),
        lax.psum_scatter(
            w_down_grad.astype(jnp.bfloat16), "seq", scatter_dimension=0, tiled=True
        ).astype(jnp.float32),
    )
    shards = (
        lax.psum_scatter(attn_gain_grad, "dp", scatter_dimension=0, tiled=True),
        lax.psum_scatter(w_query_grad, "dp", scatter_dimension=0, tiled=True),
        lax.psum_scatter(w_key_grad, "dp", scatter_dimension=0, tiled=True),
        lax.psum_scatter(w_value_grad, "dp", scatter_dimension=0, tiled=True),
        lax.psum_scatter(w_out_grad, "dp", scatter_dimension=0, tiled=True),
        lax.psum_scatter(ffn_gain_grad, "dp", scatter_dimension=0, tiled=True),
        lax.psum_scatter(w_gate_grad, "dp", scatter_dimension=0, tiled=True),
        lax.psum_scatter(w_up_grad, "dp", scatter_dimension=0, tiled=True),
        lax.psum_scatter(w_down_grad, "dp", scatter_dimension=1, tiled=True),
    )
    attn_sums = (
        lax.psum(shards[0].astype(jnp.bfloat16), "seq").astype(jnp.float32),
        lax.psum(shards[1].astype(jnp.bfloat16), "seq").astype(jnp.float32),
        lax.psum(shards[2].astype(jnp.bfloat16), "seq").astype(jnp.float32),
        lax.psum(shards[3].astype(jnp.bfloat16), "seq").astype(jnp.float32),
        lax.psum(shards[4].astype(jnp.bfloat16), "seq").astype(jnp.float32),
        lax.psum(shards[5].astype(jnp.bfloat16), "seq").astype(jnp.float32),
    )
    return (
        output,
        upstream,
        attn_sums[0],
        attn_sums[1],
        attn_sums[2],
        attn_sums[3],
        attn_sums[4],
        attn_sums[5],
        shards[6],
        shards[7],
        shards[8],
    )


def solution(mesh):
    in_specs = (
        P("dp", "seq", None),
        P("dp", "seq"),
        P("dp", "seq"),
        P(),
        P(),
        P(),
        P(),
        P(),
        P(),
        P(None, "seq"),
        P(None, "seq"),
        P("seq", None),
        P("dp", "seq", None),
    )
    out_specs = (
        P("dp", "seq", None),
        P("dp", "seq", None),
        P("dp"),
        P("dp", None),
        P("dp", None),
        P("dp", None),
        P("dp", None),
        P("dp"),
        P("dp", "seq"),
        P("dp", "seq"),
        P("seq", "dp"),
    )
    return jax.shard_map(
        on_device, mesh=mesh, in_specs=in_specs, out_specs=out_specs, check_vma=False
    )
```

profile of v0, /device:TPU:0, one launch (start us, length us, event | category | flops | bytes accessed | tf_op | source)
XLA Modules:
  0.0 1120.8 jit_solution(3167693406144594181)
XLA Ops:
  45.4 13.7 %fusion.120 = (f32[5,3,320]{2,1,0:T(4,128)S(1)}, f32[5,3,320,1280]{3,2,1,0:T(8,128)}) fusion(bf16[1280,5,64,1]{0,2,3,1:T(8,128)(2,1)} %bitcast.365, bf16[320,5,3,32]{0,3,2,1:T(8,128)(2,1)} %bitcast.385, bf16[320,5,3,32]{0,3,2,1:T(8,128)(2,1)} %bitcast.383, pred[320,1280]{1,0:T(8,128)(4,1)S(1)} %fusion.36), kind=kOutput, calls=%fused_computation.230 | convolution fusion | flops 806088000 | bytes 26438400 | tf_op jit(solution)/shard_map/while/body/eval_jaxpr/qkgd,tkd->kgqt/dot_general | solution.py:50
  59.2 12.1 %fusion.6 = f32[5,3,320]{2,1,0:T(4,128)} fusion(f32[5,3,320,1280]{3,2,1,0:T(8,128)} %get-tuple-element.172, f32[5,3,320]{2,1,0:T(4,128)S(1)} %get-tuple-element.171), kind=kLoop, calls=%fused_computation.18 | loop fusion | flops 12283200 | bytes 24614400 | tf_op jit(solution)/shard_map/while/body/eval_jaxpr/reduce_sum | solution.py:59
  92.2 25.8 %all-gather.10.cloned.1.call-done = bf16[960,2560]{1,0:T(8,128)(2,1)} async-done(((bf16[960,640]{1,0:T(8,128)(2,1)}), bf16[960,2560]{1,0:T(8,128)(2,1)}) %all-gather.10.cloned.1.call-update) | async-done | bytes 4915216 | tf_op jit(solution)/shard_map/all_gather | solution.py:122
  125.8 32.2 %all-gather.12.cloned.1.call-done = bf16[2560,960]{0,1:T(8,128)(2,1)} async-done(((bf16[640,960]{0,1:T(8,128)(2,1)}), bf16[2560,960]{0,1:T(8,128)(2,1)}) %all-gather.12.cloned.1.call-update) | async-done | bytes 4915216 | tf_op jit(solution)/shard_map/all_gather | solution.py:123
  172.3 16.2 %all-gather.14.cloned.1.call-done = bf16[1,1280,640]{2,1,0:T(8,128)(2,1)} async-done(((bf16[1,320,640]{2,1,0:T(8,128)(2,1)}), bf16[1,1280,640]{2,1,0:T(8,128)(2,1)}) %all-gather.14.cloned.1.call-update) | async-done | bytes 1638416 | tf_op jit(solution)/shard_map/all_gather | solution.py:142
  194.8 12.4 %fusion.121 = (f32[5,3,320]{2,1,0:T(4,128)}, f32[5,3,320,1280]{3,2,1,0:T(8,128)}) fusion(bf16[1280,5,64,1]{0,2,3,1:T(8,128)(2,1)S(1)} %bitcast.367, bf16[320,5,3,32]{0,3,2,1:T(8,128)(2,1)} %bitcast.389, bf16[320,5,3,32]{0,3,2,1:T(8,128)(2,1)} %bitcast.387, pred[320,1280]{1,0:T(8,128)(4,1)S(1)} %copy-done.26), kind=kOutput, calls=%fused_computation.231 | convolution fusion | flops 806088000 | bytes 26438400 | tf_op jit(solution)/shard_map/while/body/eval_jaxpr/qkgd,tkd->kgqt/dot_general | solution.py:50
  207.2 12.3 %fusion.7 = f32[5,3,320]{2,1,0:T(4,128)S(1)} fusion(f32[5,3,320,1280]{3,2,1,0:T(8,128)} %get-tuple-element.180, f32[5,3,320]{2,1,0:T(4,128)} %get-tuple-element.179), kind=kLoop, calls=%fused_computation.19 | loop fusion | flops 12283200 | bytes 24614400 | tf_op jit(solution)/shard_map/while/body/eval_jaxpr/reduce_sum | solution.py:59
  252.1 9.8 fusion.28
  262.0 19.4 %fusion.3 = (f32[5,3,320]{2,1,0:T(4,128)S(1)}, f32[5,1280,320,3]{1,2,3,0:T(8,128)}) fusion(f32[5,3,320,1280]{3,2,1,0:T(8,128)} %get-tuple-element.180, f32[5,3,320]{2,1,0:T(4,128)S(1)} %copy-done.66, bf16[1280,5,64,1]{0,2,3,1:T(8,128)(2,1)S(1)} %bitcast.394, bf16[320,5,3,64]{0,3,2,1:T(8,128)(2,1)S(1)} %bitcast.372), kind=kOutput, calls=%fused_computation.7 | convolution fusion | flops 804859200 | bytes 50624000 | tf_op jit(solution)/shard_map/while/body/eval_jaxpr/qkgd,tkd->kgqt/dot_general | solution.py:71
  281.4 16.4 %fusion.5 = bf16[5,3,320,1280]{3,2,1,0:T(8,128)(2,1)S(1)} fusion(f32[5,1280,320,3]{1,2,3,0:T(8,128)} %get-tuple-element.185, f32[5,3,320,1280]{3,2,1,0:T(8,128)} %get-tuple-element.180, f32[5,3,320]{2,1,0:T(4,128)S(1)} %get-tuple-element.184, f32[5,3,320]{2,1,0:T(4,128)S(1)} %copy-done.66), kind=kLoop, calls=%fused_computation.9 | loop fusion | flops 24576000 | bytes 61478400 | tf_op jit(solution)/shard_map/while/body/eval_jaxpr/convert_element_type | solution.py:75
  324.9 18.4 %reduce-scatter.33.cloned.1.call-done = bf16[320,640]{1,0:T(8,128)(2,1)} async-done(((bf16[1280,640]{1,0:T(8,128)(2,1)}), bf16[320,640]{1,0:T(8,128)(2,1)}) %reduce-scatter.33.cloned.1.call-update) | async-done | bytes 409616
  371.9 9.8 fusion.31
  381.7 19.4 %fusion = (f32[5,3,320]{2,1,0:T(4,128)S(1)}, f32[5,1280,320,3]{1,2,3,0:T(8,128)}) fusion(f32[5,3,320,1280]{3,2,1,0:T(8,128)} %get-tuple-element.172, f32[5,3,320]{2,1,0:T(4,128)S(1)} %copy-done.65, bf16[1280,5,64,1]{0,2,3,1:T(8,128)(2,1)S(1)} %bitcast.392, bf16[320,5,3,64]{0,3,2,1:T(8,128)(2,1)S(1)} %bitcast.374), kind=kOutput, calls=%fused_computation.2 | convolution fusion | flops 804859200 | bytes 50624000 | tf_op jit(solution)/shard_map/while/body/eval_jaxpr/qkgd,tkd->kgqt/dot_general | solution.py:71
  401.1 16.4 %fusion.2 = bf16[5,3,320,1280]{3,2,1,0:T(8,128)(2,1)S(1)} fusion(f32[5,1280,320,3]{1,2,3,0:T(8,128)} %get-tuple-element.189, f32[5,3,320,1280]{3,2,1,0:T(8,128)} %get-tuple-element.172, f32[5,3,320]{2,1,0:T(4,128)S(1)} %get-tuple-element.188, f32[5,3,320]{2,1,0:T(4,128)S(1)} %copy-done.65), kind=kLoop, calls=%fused_computation.4 | loop fusion | flops 24576000 | bytes 61478400 | tf_op jit(solution)/shard_map/while/body/eval_jaxpr/convert_element_type | solution.py:75
  437.8 9.0 convolution_multiply_fusion
  533.5 134.0 %all-reduce.15 = (bf16[960]{0:T(1024)(128)(2,1)S(1)}, bf16[960,320]{0,1:T(8,128)(2,1)S(1)}, bf16[960,320]{0,1:T(8,128)(2,1)}, bf16[960]{0:T(1024)(128)(2,1)S(1)}) all-reduce(f32[960]{0:T(1024)S(1)} %add.284, f32[960,320]{0,1:T(8,128)} %convolution_add_fusion.5, ...), channel_id=4, replica_groups=mesh['seq'=4,'dp'=8] {'dp'}, use_global_device_ids=true, to_apply=%region_18.19.clone | all-reduce | flops 616320 | bytes 3697920
  670.9 23.2 %reduce-scatter.31.cloned.1.call-done = f32[120,960]{1,0:T(8,128)} async-done(((f32[960,960]{1,0:T(8,128)}), f32[120,960]{1,0:T(8,128)}) %reduce-scatter.31.cloned.1.call-update) | async-done | bytes 460816 | tf_op jit(solution)/shard_map/reduce_scatter | solution.py:301
  696.0 51.7 %reduce-scatter.37.cloned.1.call-done = bf16[640,960]{1,0:T(8,128)(2,1)} async-done(((bf16[2560,960]{1,0:T(8,128)(2,1)}), bf16[640,960]{1,0:T(8,128)(2,1)}) %reduce-scatter.37.cloned.1.call-update) | async-done | bytes 1228816
  753.0 48.8 %reduce-scatter.39.cloned.1.call-done = bf16[640,960]{1,0:T(8,128)(2,1)} async-done(((bf16[2560,960]{1,0:T(8,128)(2,1)}), bf16[640,960]{1,0:T(8,128)(2,1)}) %reduce-scatter.39.cloned.1.call-update) | async-done | bytes 1228816
  807.1 48.4 %reduce-scatter.41.cloned.1.call-done = bf16[640,960]{1,0:T(8,128)(2,1)} async-done(((bf16[2560,960]{1,0:T(8,128)(2,1)}), bf16[640,960]{1,0:T(8,128)(2,1)}) %reduce-scatter.41.cloned.1.call-update) | async-done | bytes 1228816
  877.4 15.7 %all-reduce.14.cloned.1.call-done = (bf16[120,960]{1,0:T(8,128)(2,1)}, bf16[120,320]{0,1:T(8,128)(2,1)}, bf16[120,320]{0,1:T(8,128)(2,1)}, bf16[120,960]{1,0:T(8,128)(2,1)}) async-done(((bf16[120,960]{1,0:T(8,128)(2,1)}, bf16[120,320]{0,1:T(8,128)(2,1)}, bf16[120,320]{0,1:T(8,128)(2,1)}, bf16[120,960]{1,0:T(8,128)(2,1)}), (bf16[120,960]{1,0:T(8,128)(2,1)}, bf16[120,320]{0,1:T(8,128)(2,1)}, ...) | async-done | bytes 614416 | tf_op jit(solution)/shard_map/psum | solution.py:309
  899.8 67.6 %reduce-scatter.43.cloned.1.call-done = f32[120,640]{1,0:T(8,128)} async-done(((f32[960,640]{1,0:T(8,128)}), f32[120,640]{1,0:T(8,128)}) %reduce-scatter.43.cloned.1.call-update) | async-done | bytes 307216
  967.4 73.3 %reduce-scatter.45.cloned.1.call-done = f32[120,640]{1,0:T(8,128)} async-done(((f32[960,640]{1,0:T(8,128)}), f32[120,640]{1,0:T(8,128)}) %reduce-scatter.45.cloned.1.call-update) | async-done | bytes 307216
  1040.6 73.2 %reduce-scatter.47.cloned.1.call-done = f32[640,120]{0,1:T(8,128)} async-done(((f32[640,960]{0,1:T(8,128)}), f32[640,120]{0,1:T(8,128)}) %reduce-scatter.47.cloned.1.call-update) | async-done | bytes 307216
  (394 shorter events, 324.2 us)
Async XLA Ops:
  7.2 74.2 %copy-start = (bf16[960,960]{1,0:T(8,128)(2,1)S(1)}, bf16[960,960]{1,0:T(8,128)(2,1)}, u32[]{:S(2)}) copy-start(bf16[960,960]{1,0:T(8,128)(2,1)} %param.20) | copy-start | bytes 5529604
  7.2 30.5 %all-gather.6.cloned.1.call-start = ((), (), s32[]{:S(2)}) async-start(), calls=%async_computation.10 | async-start | bytes 2048000 | tf_op jit(solution)/shard_map/all_gather | solution.py:142
  13.4 157.7 %copy-start.35 = (f32[320,32]{0,1:T(8,128)}, f32[320,32]{0,1:T(8,128)S(1)}, u32[]{:S(2)}) copy-start(f32[320,32]{0,1:T(8,128)S(1)} %get-tuple-element.162) | copy-start | bytes 122884
  14.7 70.1 %all-gather.8.cloned.1.call-start = ((), (), s32[]{:S(2)}) async-start(), calls=%async_computation.11 | async-start | bytes 6144000 | tf_op jit(solution)/shard_map/all_gather | solution.py:121
  15.4 102.6 %all-gather.10.cloned.1.call-start = ((), (), s32[]{:S(2)}) async-start(), calls=%async_computation.12 | async-start | bytes 6144000 | tf_op jit(solution)/shard_map/all_gather | solution.py:122
  16.2 141.8 %all-gather.12.cloned.1.call-start = ((), (), s32[]{:S(2)}) async-start(), calls=%async_computation.13 | async-start | bytes 6144000 | tf_op jit(solution)/shard_map/all_gather | solution.py:123
  16.7 171.8 %all-gather.14.cloned.1.call-start = ((), (), s32[]{:S(2)}) async-start(), calls=%async_computation.14 | async-start | bytes 2048000 | tf_op jit(solution)/shard_map/all_gather | solution.py:142
  92.2 65.8 %copy-start.13 = (f32[1,320,960]{2,1,0:T(8,128)S(1)}, f32[1,320,960]{2,1,0:T(8,128)}, u32[]{:S(2)}) copy-start(f32[1,320,960]{2,1,0:T(8,128)} %copy-done.12) | copy-start | bytes 3686404
  168.4 174.9 %reduce-scatter.33.cloned.1.call-start = ((), (), s32[]{:S(2)}) async-start(), calls=%async_computation.17 | async-start | bytes 2048000
  281.4 16.4 %copy-start.40 = (bf16[1,320,15,32]{1,3,2,0:T(8,128)(2,1)S(1)}, bf16[1,320,15,32]{1,3,2,0:T(8,128)(2,1)}, u32[]{:S(2)}) copy-start(bf16[1,320,15,32]{1,3,2,0:T(8,128)(2,1)} %get-tuple-element.144) | copy-start | bytes 921604
  281.4 16.4 %copy-start.41 = (bf16[1,320,15,32]{1,3,2,0:T(8,128)(2,1)S(1)}, bf16[1,320,15,32]{1,3,2,0:T(8,128)(2,1)}, u32[]{:S(2)}) copy-start(bf16[1,320,15,32]{1,3,2,0:T(8,128)(2,1)} %get-tuple-element.145) | copy-start | bytes 921604
  314.5 201.0 %reduce-scatter.35.cloned.1.call-start = ((), (), s32[]{:S(2)}) async-start(), calls=%async_computation.18 | async-start | bytes 2048000
  324.9 28.7 %copy-start.47 = (bf16[1,320,15,64]{1,3,2,0:T(8,128)(2,1)}, bf16[1,320,15,64]{1,3,2,0:T(8,128)(2,1)S(1)}, u32[]{:S(2)}) copy-start(bf16[1,320,15,64]{1,3,2,0:T(8,128)(2,1)S(1)} %maximum_convert_fusion) | copy-start | bytes 1843204
  401.1 16.4 %copy-start.38 = (bf16[1,320,15,32]{1,3,2,0:T(8,128)(2,1)S(1)}, bf16[1,320,15,32]{1,3,2,0:T(8,128)(2,1)}, u32[]{:S(2)}) copy-start(bf16[1,320,15,32]{1,3,2,0:T(8,128)(2,1)} %get-tuple-element.146) | copy-start | bytes 921604
  401.1 16.4 %copy-start.39 = (bf16[1,320,15,32]{1,3,2,0:T(8,128)(2,1)S(1)}, bf16[1,320,15,32]{1,3,2,0:T(8,128)(2,1)}, u32[]{:S(2)}) copy-start(bf16[1,320,15,32]{1,3,2,0:T(8,128)(2,1)} %get-tuple-element.147) | copy-start | bytes 921604
  434.3 234.9 %reduce-scatter.29.cloned.1.call-start = ((), (), s32[]{:S(2)}) async-start(), calls=%async_computation.15 | async-start | bytes 4423680 | tf_op jit(solution)/shard_map/reduce_scatter | solution.py:298
  451.5 242.6 %reduce-scatter.31.cloned.1.call-start = ((), (), s32[]{:S(2)}) async-start(), calls=%async_computation.16 | async-start | bytes 4423680 | tf_op jit(solution)/shard_map/reduce_scatter | solution.py:301
  457.6 290.0 %reduce-scatter.37.cloned.1.call-start = ((), (), s32[]{:S(2)}) async-start(), calls=%async_computation.19 | async-start | bytes 6553600
  475.1 326.6 %reduce-scatter.39.cloned.1.call-start = ((), (), s32[]{:S(2)}) async-start(), calls=%async_computation.20 | async-start | bytes 6553600
  492.3 363.2 %reduce-scatter.41.cloned.1.call-start = ((), (), s32[]{:S(2)}) async-start(), calls=%async_computation.21 | async-start | bytes 6553600
  509.6 383.5 %all-reduce.14.cloned.1.call-start = ((), (), s32[]{:S(2)}) async-start(), calls=%async_computation.25 | async-start | bytes 1310720 | tf_op jit(solution)/shard_map/psum | solution.py:309
  695.9 271.5 %reduce-scatter.43.cloned.1.call-start = ((), (), s32[]{:S(2)}) async-start(), calls=%async_computation.22 | async-start | bytes 2764800
  752.9 287.7 %reduce-scatter.45.cloned.1.call-start = ((), (), s32[]{:S(2)}) async-start(), calls=%async_computation.23 | async-start | bytes 2764800
  807.1 306.8 %reduce-scatter.47.cloned.1.call-start = ((), (), s32[]{:S(2)}) async-start(), calls=%async_computation.24 | async-start | bytes 2764800
  (97 other events, 418.2 us)
Sparse Core Ops, SparseCore 0:
  14.8 22.8 all-gather.5
  39.3 38.5 all-gather.7
  79.4 38.5 all-gather.9
  119.4 38.5 all-gather.11
  168.5 20.0 all-gather.13
  314.7 28.5 reduce-scatter.32
  434.4 28.5 reduce-scatter.34
  466.7 89.4 reduce-scatter.28
  560.3 133.7 reduce-scatter.30
  696.5 51.0 reduce-scatter.36
  750.4 51.3 reduce-scatter.38
  804.1 51.3 reduce-scatter.40
  858.8 34.2 all-reduce.13
  897.6 69.7 reduce-scatter.42
  971.9 68.7 reduce-scatter.44
  1045.1 68.6 reduce-scatter.46
where the time goes:
time: 1130 us; the launch traced here: 1120 us
  waiting for transfers between devices  501 us (44%)
  matrix products  243 us (22%)
  blocking collectives  147 us (13%)
  local copies, waits for them, and re-layouts  111 us (10%)
  other arithmetic  100 us (9%)
  between operations  17.3 us (2%)
    unnamed x24, waiting for transfers between devices  383 us
    unnamed x2, blocking collectives  141 us
    unnamed x233, local copies, waits for them, and re-layouts  88.9 us
    dot_general x2, matrix products, row_backward(): jnp.einsum('qkgd,tkd->kgqt', mixed_grad, values_all, preferred_element_ty...  38.8 us
    convert_element_type x2, other arithmetic, row_backward(): score_grad = (weights_soft * (probs_grad - row_delta)).astype(jnp.bfloat16)  32.7 us
    all_gather x1, waiting for transfers between devices, on_device(): lax.all_gather(w_down, 'seq', axis=0, tiled=True)  32.2 us
    dot_general x2, matrix products, masked_scores(): jnp.einsum('qkgd,tkd->kgqt', queries, keys_all, preferred_element_type=jn...  26.1 us
    all_gather x1, waiting for transfers between devices, on_device(): lax.all_gather(w_up, 'seq', axis=1, tiled=True)  25.8 us
  transfers between devices with their start and end apart: 16, of which 13 were waited for; matrix products, arithmetic and copies ran while one was open for 19% of the time, Pallas kernels for 0%

commit v1 on v0

--- a/solution.py
+++ b/solution.py
@@ -1,3 +1,4 @@
+import functools
 import jax
 import jax.numpy as jnp
 from jax import lax
@@ -9,6 +10,15 @@
 EPSILON = 1e-05
 THETA = 10000.0
 MASKED = -1e30
+
+
+def _wrap_stops_all(mine, which_dim):
+    w_next = jnp.stack([mine for _ in range(lax.axis_size("seq"))], 0)
+    work_now = lax.all_to_all(w_next, "seq", 0, 0)
+    return jnp.concatenate(work_now, which_dim)
+
+
+expand_block = functools.partial(_wrap_stops_all, which_dim=1)
 
 
 def rope_tables(positions):
@@ -119,7 +129,7 @@
     cos_table, sin_table = rope_tables(positions)
     gate_mat, up_mat, down_mat = (
         lax.all_gather(w_gate, "seq", axis=1, tiled=True),
-        lax.all_gather(w_up, "seq", axis=1, tiled=True),
+        expand_block(w_up),
         lax.all_gather(w_down, "seq", axis=0, tiled=True),
     )
     residual = tokens.astype(jnp.float32)

time: 1130 us -> 1150 us (1.018)
  blocking collectives: 147 us -> 221 us
  waiting for transfers between devices: 501 us -> 439 us
    unnamed x2, blocking collectives: 141 us -> 215 us
    all_gather x1, waiting for transfers between devices: 32.2 us -> 0.01 us  [on_device(): lax.all_gather(w_down, 'seq', axis=0, tiled=True)]
    all_gather x1 -> x0, waiting for transfers between devices: 25.8 us -> none  [on_device(): lax.all_gather(w_up, 'seq', axis=1, tiled=True)]
    unnamed x233 -> x235, local copies, waits for them, and re-layouts: 88.9 us -> 89.6 us
    unnamed x24 -> x23, waiting for transfers between devices: 383 us -> 383 us
  transfers between devices with their start and end apart: 16 -> 16, of which waited for: 13 -> 10; matrix products, arithmetic and copies ran while one was open for 19% -> 19% of each run, Pallas kernels for 0% -> 0%
where the time goes in v1:
time: 1150 us; the launch traced here: 1140 us
  waiting for transfers between devices  439 us (38%)
  matrix products  239 us (21%)
  blocking collectives  221 us (19%)
  local copies, waits for them, and re-layouts  122 us (11%)
  other arithmetic  101 us (9%)
  between operations  17.3 us (2%)
    unnamed x23, waiting for transfers between devices  383 us
    unnamed x2, blocking collectives  215 us
    unnamed x235, local copies, waits for them, and re-layouts  89.6 us
    dot_general x2, matrix products, row_backward(): jnp.einsum('qkgd,tkd->kgqt', mixed_grad, values_all, preferred_element_ty...  38.8 us
    convert_element_type x2, other arithmetic, row_backward(): score_grad = (weights_soft * (probs_grad - row_delta)).astype(jnp.bfloat16)  32.9 us
    dot_general x2, matrix products, masked_scores(): jnp.einsum('qkgd,tkd->kgqt', queries, keys_all, preferred_element_type=jn...  25.9 us
    reduce_sum x2, other arithmetic, row_attend(): row_total = jnp.sum(shifted, axis=-1, keepdims=True)  24.5 us
    reduce_scatter x1, waiting for transfers between devices, on_device(): lax.psum_scatter(w_out_grad, 'dp', scatter_dimension=0, tiled=True)  23.9 us
  transfers between devices with their start and end apart: 16, of which 10 were waited for; matrix products, arithmetic and copies ran while one was open for 19% of the time, Pallas kernels for 0%

profile of v1, /device:TPU:0, one launch (start us, length us, event | category | flops | bytes accessed | tf_op | source)
XLA Modules:
  0.0 1144.5 jit_solution(10415840720253636638)
XLA Ops:
  34.4 81.0 %all-reduce = s32[1280]{0:T(1024)S(1)} all-reduce(s32[1280]{0:T(1024)S(1)} %dynamic-update-slice), channel_id=1, replica_groups=mesh['seq'=4,'dp'=8] {'seq'}, use_global_device_ids=true, to_apply=%add | all-reduce | flops 1280 | bytes 10240
  124.2 13.6 %fusion.120 = (f32[5,3,320]{2,1,0:T(4,128)S(1)}, f32[5,3,320,1280]{3,2,1,0:T(8,128)}) fusion(bf16[1280,5,64,1]{0,2,3,1:T(8,128)(2,1)} %bitcast.368, bf16[320,5,3,32]{0,3,2,1:T(8,128)(2,1)} %bitcast.396, bf16[320,5,3,32]{0,3,2,1:T(8,128)(2,1)} %bitcast.394, pred[320,1280]{1,0:T(8,128)(4,1)S(1)} %fusion.36), kind=kOutput, calls=%fused_computation.230 | convolution fusion | flops 806088000 | bytes 26438400 | tf_op jit(solution)/shard_map/while/body/eval_jaxpr/qkgd,tkd->kgqt/dot_general | solution.py:60
  137.8 12.0 %fusion.6 = f32[5,3,320]{2,1,0:T(4,128)} fusion(f32[5,3,320,1280]{3,2,1,0:T(8,128)} %get-tuple-element.172, f32[5,3,320]{2,1,0:T(4,128)S(1)} %get-tuple-element.171), kind=kLoop, calls=%fused_computation.18 | loop fusion | flops 12283200 | bytes 24614400 | tf_op jit(solution)/shard_map/while/body/eval_jaxpr/reduce_sum | solution.py:69
  194.7 16.1 %all-gather.11.cloned.1.call-done = bf16[1,1280,640]{2,1,0:T(8,128)(2,1)} async-done(((bf16[1,320,640]{2,1,0:T(8,128)(2,1)}), bf16[1,1280,640]{2,1,0:T(8,128)(2,1)}) %all-gather.11.cloned.1.call-update) | async-done | bytes 1638416 | tf_op jit(solution)/shard_map/all_gather | solution.py:152
  217.0 12.3 %fusion.121 = (f32[5,3,320]{2,1,0:T(4,128)}, f32[5,3,320,1280]{3,2,1,0:T(8,128)}) fusion(bf16[1280,5,64,1]{0,2,3,1:T(8,128)(2,1)S(1)} %bitcast.370, bf16[320,5,3,32]{0,3,2,1:T(8,128)(2,1)} %bitcast.400, bf16[320,5,3,32]{0,3,2,1:T(8,128)(2,1)} %bitcast.398, pred[320,1280]{1,0:T(8,128)(4,1)S(1)} %copy-done.26), kind=kOutput, calls=%fused_computation.231 | convolution fusion | flops 806088000 | bytes 26438400 | tf_op jit(solution)/shard_map/while/body/eval_jaxpr/qkgd,tkd->kgqt/dot_general | solution.py:60
  229.4 12.5 %fusion.7 = f32[5,3,320]{2,1,0:T(4,128)S(1)} fusion(f32[5,3,320,1280]{3,2,1,0:T(8,128)} %get-tuple-element.180, f32[5,3,320]{2,1,0:T(4,128)} %get-tuple-element.179), kind=kLoop, calls=%fused_computation.19 | loop fusion | flops 12283200 | bytes 24614400 | tf_op jit(solution)/shard_map/while/body/eval_jaxpr/reduce_sum | solution.py:69
  274.3 9.8 fusion.28
  284.1 19.4 %fusion.3 = (f32[5,3,320]{2,1,0:T(4,128)S(1)}, f32[5,1280,320,3]{1,2,3,0:T(8,128)}) fusion(f32[5,3,320,1280]{3,2,1,0:T(8,128)} %get-tuple-element.180, f32[5,3,320]{2,1,0:T(4,128)S(1)} %copy-done.67, bf16[1280,5,64,1]{0,2,3,1:T(8,128)(2,1)S(1)} %bitcast.405, bf16[320,5,3,64]{0,3,2,1:T(8,128)(2,1)S(1)} %bitcast.375), kind=kOutput, calls=%fused_computation.7 | convolution fusion | flops 804859200 | bytes 50624000 | tf_op jit(solution)/shard_map/while/body/eval_jaxpr/qkgd,tkd->kgqt/dot_general | solution.py:81
  303.6 16.4 %fusion.5 = bf16[5,3,320,1280]{3,2,1,0:T(8,128)(2,1)S(1)} fusion(f32[5,1280,320,3]{1,2,3,0:T(8,128)} %get-tuple-element.185, f32[5,3,320,1280]{3,2,1,0:T(8,128)} %get-tuple-element.180, f32[5,3,320]{2,1,0:T(4,128)S(1)} %get-tuple-element.184, f32[5,3,320]{2,1,0:T(4,128)S(1)} %copy-done.67), kind=kLoop, calls=%fused_computation.9 | loop fusion | flops 24576000 | bytes 61478400 | tf_op jit(solution)/shard_map/while/body/eval_jaxpr/convert_element_type | solution.py:85
  338.1 8.6 convolution_multiply_fusion.1
  347.1 18.4 %reduce-scatter.33.cloned.1.call-done = bf16[320,640]{1,0:T(8,128)(2,1)} async-done(((bf16[1280,640]{1,0:T(8,128)(2,1)}), bf16[320,640]{1,0:T(8,128)(2,1)}) %reduce-scatter.33.cloned.1.call-update) | async-done | bytes 409616
  394.7 9.8 fusion.31
  404.6 19.4 %fusion = (f32[5,3,320]{2,1,0:T(4,128)S(1)}, f32[5,1280,320,3]{1,2,3,0:T(8,128)}) fusion(f32[5,3,320,1280]{3,2,1,0:T(8,128)} %get-tuple-element.172, f32[5,3,320]{2,1,0:T(4,128)S(1)} %copy-done.66, bf16[1280,5,64,1]{0,2,3,1:T(8,128)(2,1)S(1)} %bitcast.403, bf16[320,5,3,64]{0,3,2,1:T(8,128)(2,1)S(1)} %bitcast.377), kind=kOutput, calls=%fused_computation.2 | convolution fusion | flops 804859200 | bytes 50624000 | tf_op jit(solution)/shard_map/while/body/eval_jaxpr/qkgd,tkd->kgqt/dot_general | solution.py:81
  424.0 16.5 %fusion.2 = bf16[5,3,320,1280]{3,2,1,0:T(8,128)(2,1)S(1)} fusion(f32[5,1280,320,3]{1,2,3,0:T(8,128)} %get-tuple-element.189, f32[5,3,320,1280]{3,2,1,0:T(8,128)} %get-tuple-element.172, f32[5,3,320]{2,1,0:T(4,128)S(1)} %get-tuple-element.188, f32[5,3,320]{2,1,0:T(4,128)S(1)} %copy-done.66), kind=kLoop, calls=%fused_computation.4 | loop fusion | flops 24576000 | bytes 61478400 | tf_op jit(solution)/shard_map/while/body/eval_jaxpr/convert_element_type | solution.py:85
  460.9 9.0 convolution_multiply_fusion
  556.5 133.7 %all-reduce.15 = (bf16[960]{0:T(1024)(128)(2,1)S(1)}, bf16[960,320]{0,1:T(8,128)(2,1)S(1)}, bf16[960,320]{0,1:T(8,128)(2,1)}, bf16[960]{0:T(1024)(128)(2,1)S(1)}) all-reduce(f32[960]{0:T(1024)S(1)} %add.284, f32[960,320]{0,1:T(8,128)} %convolution_add_fusion.5, ...), channel_id=4, replica_groups=mesh['seq'=4,'dp'=8] {'dp'}, use_global_device_ids=true, to_apply=%region_18.19.clone | all-reduce | flops 616320 | bytes 3697920
  693.7 23.9 %reduce-scatter.31.cloned.1.call-done = f32[120,960]{1,0:T(8,128)} async-done(((f32[960,960]{1,0:T(8,128)}), f32[120,960]{1,0:T(8,128)}) %reduce-scatter.31.cloned.1.call-update) | async-done | bytes 460816 | tf_op jit(solution)/shard_map/reduce_scatter | solution.py:311
  719.5 51.8 %reduce-scatter.37.cloned.1.call-done = bf16[640,960]{1,0:T(8,128)(2,1)} async-done(((bf16[2560,960]{1,0:T(8,128)(2,1)}), bf16[640,960]{1,0:T(8,128)(2,1)}) %reduce-scatter.37.cloned.1.call-update) | async-done | bytes 1228816
  776.6 48.6 %reduce-scatter.39.cloned.1.call-done = bf16[640,960]{1,0:T(8,128)(2,1)} async-done(((bf16[2560,960]{1,0:T(8,128)(2,1)}), bf16[640,960]{1,0:T(8,128)(2,1)}) %reduce-scatter.39.cloned.1.call-update) | async-done | bytes 1228816
  830.6 48.6 %reduce-scatter.41.cloned.1.call-done = bf16[640,960]{1,0:T(8,128)(2,1)} async-done(((bf16[2560,960]{1,0:T(8,128)(2,1)}), bf16[640,960]{1,0:T(8,128)(2,1)}) %reduce-scatter.41.cloned.1.call-update) | async-done | bytes 1228816
  901.0 15.5 %all-reduce.14.cloned.1.call-done = (bf16[120,960]{1,0:T(8,128)(2,1)}, bf16[120,320]{0,1:T(8,128)(2,1)}, bf16[120,320]{0,1:T(8,128)(2,1)}, bf16[120,960]{1,0:T(8,128)(2,1)}) async-done(((bf16[120,960]{1,0:T(8,128)(2,1)}, bf16[120,320]{0,1:T(8,128)(2,1)}, bf16[120,320]{0,1:T(8,128)(2,1)}, bf16[120,960]{1,0:T(8,128)(2,1)}), (bf16[120,960]{1,0:T(8,128)(2,1)}, bf16[120,320]{0,1:T(8,128)(2,1)}, ...) | async-done | bytes 614416 | tf_op jit(solution)/shard_map/psum | solution.py:319
  923.2 67.8 %reduce-scatter.43.cloned.1.call-done = f32[120,640]{1,0:T(8,128)} async-done(((f32[960,640]{1,0:T(8,128)}), f32[120,640]{1,0:T(8,128)}) %reduce-scatter.43.cloned.1.call-update) | async-done | bytes 307216
  991.0 73.2 %reduce-scatter.45.cloned.1.call-done = f32[120,640]{1,0:T(8,128)} async-done(((f32[960,640]{1,0:T(8,128)}), f32[120,640]{1,0:T(8,128)}) %reduce-scatter.45.cloned.1.call-update) | async-done | bytes 307216
  1064.3 73.3 %reduce-scatter.47.cloned.1.call-done = f32[640,120]{0,1:T(8,128)} async-done(((f32[640,960]{0,1:T(8,128)}), f32[640,120]{0,1:T(8,128)}) %reduce-scatter.47.cloned.1.call-update) | async-done | bytes 307216
  (396 shorter events, 315.8 us)
Async XLA Ops:
  7.2 152.8 %copy-start = (bf16[960,960]{1,0:T(8,128)(2,1)S(1)}, bf16[960,960]{1,0:T(8,128)(2,1)}, u32[]{:S(2)}) copy-start(bf16[960,960]{1,0:T(8,128)(2,1)} %param.20) | copy-start | bytes 5529604
  7.2 108.8 %all-gather.5.cloned.1.call-start = ((), (), s32[]{:S(2)}) async-start(), calls=%async_computation.11 | async-start | bytes 2048000 | tf_op jit(solution)/shard_map/all_gather | solution.py:152
  9.3 19.6 %copy-start.76 = (f32[320]{0:T(512)}, f32[320]{0:T(512)S(1)}, u32[]{:S(2)}) copy-start(f32[320]{0:T(512)S(1)} %get-tuple-element.164) | copy-start | bytes 3844
  13.5 180.0 %copy-start.36 = (f32[320,32]{0,1:T(8,128)}, f32[320,32]{0,1:T(8,128)S(1)}, u32[]{:S(2)}) copy-start(f32[320,32]{0,1:T(8,128)S(1)} %get-tuple-element.162) | copy-start | bytes 122884
  14.7 154.0 %all-gather.7.cloned.1.call-start = ((), (), s32[]{:S(2)}) async-start(), calls=%async_computation.12 | async-start | bytes 6144000 | tf_op jit(solution)/shard_map/all_gather | solution.py:131
  19.3 144.1 %all-to-all-start = ((bf16[4,960,640]{2,1,0:T(8,128)(2,1)}), bf16[4,960,640]{2,1,0:T(8,128)(2,1)}, u32[]{:S(2)}, u32[]{:S(2)}) async-start(bf16[4,960,640]{2,1,0:T(8,128)(2,1)} %stack.2), calls=%async_computation | async-start | bytes 9830400 | tf_op jit(solution)/shard_map/all_to_all | solution.py:17
  24.2 156.1 %all-gather.9.cloned.1.call-start = ((), (), s32[]{:S(2)}) async-start(), calls=%async_computation.13 | async-start | bytes 6144000 | tf_op jit(solution)/shard_map/all_gather | solution.py:133
  25.0 185.8 %all-gather.11.cloned.1.call-start = ((), (), s32[]{:S(2)}) async-start(), calls=%async_computation.14 | async-start | bytes 2048000 | tf_op jit(solution)/shard_map/all_gather | solution.py:152
  190.7 174.7 %reduce-scatter.33.cloned.1.call-start = ((), (), s32[]{:S(2)}) async-start(), calls=%async_computation.17 | async-start | bytes 2048000
  303.5 16.4 %copy-start.41 = (bf16[1,320,15,32]{1,3,2,0:T(8,128)(2,1)S(1)}, bf16[1,320,15,32]{1,3,2,0:T(8,128)(2,1)}, u32[]{:S(2)}) copy-start(bf16[1,320,15,32]{1,3,2,0:T(8,128)(2,1)} %get-tuple-element.144) | copy-start | bytes 921604
  303.6 16.4 %copy-start.42 = (bf16[1,320,15,32]{1,3,2,0:T(8,128)(2,1)S(1)}, bf16[1,320,15,32]{1,3,2,0:T(8,128)(2,1)}, u32[]{:S(2)}) copy-start(bf16[1,320,15,32]{1,3,2,0:T(8,128)(2,1)} %get-tuple-element.145) | copy-start | bytes 921604
  336.7 201.9 %reduce-scatter.35.cloned.1.call-start = ((), (), s32[]{:S(2)}) async-start(), calls=%async_computation.18 | async-start | bytes 2048000
  347.1 28.7 %copy-start.48 = (bf16[1,320,15,64]{1,3,2,0:T(8,128)(2,1)}, bf16[1,320,15,64]{1,3,2,0:T(8,128)(2,1)S(1)}, u32[]{:S(2)}) copy-start(bf16[1,320,15,64]{1,3,2,0:T(8,128)(2,1)S(1)} %maximum_convert_fusion) | copy-start | bytes 1843204
  424.0 16.6 %copy-start.39 = (bf16[1,320,15,32]{1,3,2,0:T(8,128)(2,1)S(1)}, bf16[1,320,15,32]{1,3,2,0:T(8,128)(2,1)}, u32[]{:S(2)}) copy-start(bf16[1,320,15,32]{1,3,2,0:T(8,128)(2,1)} %get-tuple-element.146) | copy-start | bytes 921604
  424.0 16.6 %copy-start.40 = (bf16[1,320,15,32]{1,3,2,0:T(8,128)(2,1)S(1)}, bf16[1,320,15,32]{1,3,2,0:T(8,128)(2,1)}, u32[]{:S(2)}) copy-start(bf16[1,320,15,32]{1,3,2,0:T(8,128)(2,1)} %get-tuple-element.147) | copy-start | bytes 921604
  457.3 234.7 %reduce-scatter.29.cloned.1.call-start = ((), (), s32[]{:S(2)}) async-start(), calls=%async_computation.15 | async-start | bytes 4423680 | tf_op jit(solution)/shard_map/reduce_scatter | solution.py:308
  474.5 243.1 %reduce-scatter.31.cloned.1.call-start = ((), (), s32[]{:S(2)}) async-start(), calls=%async_computation.16 | async-start | bytes 4423680 | tf_op jit(solution)/shard_map/reduce_scatter | solution.py:311
  480.7 290.6 %reduce-scatter.37.cloned.1.call-start = ((), (), s32[]{:S(2)}) async-start(), calls=%async_computation.19 | async-start | bytes 6553600
  498.1 327.1 %reduce-scatter.39.cloned.1.call-start = ((), (), s32[]{:S(2)}) async-start(), calls=%async_computation.20 | async-start | bytes 6553600
  515.3 363.9 %reduce-scatter.41.cloned.1.call-start = ((), (), s32[]{:S(2)}) async-start(), calls=%async_computation.21 | async-start | bytes 6553600
  532.6 384.0 %all-reduce.14.cloned.1.call-start = ((), (), s32[]{:S(2)}) async-start(), calls=%async_computation.25 | async-start | bytes 1310720 | tf_op jit(solution)/shard_map/psum | solution.py:319
  719.5 271.6 %reduce-scatter.43.cloned.1.call-start = ((), (), s32[]{:S(2)}) async-start(), calls=%async_computation.22 | async-start | bytes 2764800
  776.6 287.7 %reduce-scatter.45.cloned.1.call-start = ((), (), s32[]{:S(2)}) async-start(), calls=%async_computation.23 | async-start | bytes 2764800
  830.5 307.0 %reduce-scatter.47.cloned.1.call-start = ((), (), s32[]{:S(2)}) async-start(), calls=%async_computation.24 | async-start | bytes 2764800
  (98 other events, 428.2 us)
Sparse Core Ops, SparseCore 0:
  14.8 30.8 all-gather.4
  47.3 64.0 all-gather.6
  113.0 38.5 all-gather.8
  190.8 19.8 all-gather.10
  336.8 28.5 reduce-scatter.32
  457.4 28.5 reduce-scatter.34
  489.8 89.2 reduce-scatter.28
  583.2 134.4 reduce-scatter.30
  720.2 51.0 reduce-scatter.36
  773.8 51.3 reduce-scatter.38
  827.8 51.3 reduce-scatter.40
  882.3 34.1 all-reduce.13
  921.2 69.7 reduce-scatter.42
  995.5 68.6 reduce-scatter.44
  1068.7 68.7 reduce-scatter.46
